TPU v7x, 32 devices: a whole 2x2x4 slice. The times are simulated.
32 devices in a mesh: tile: 8 (over z, x), depth: 4 (over y, core).
Axes of the slice: x: 2, y: 2, z: 4, core: 2. Of those that a mesh axis runs over, the one named last changes fastest.
Arguments:
- density: float32 [64, 128, 128], P('depth', 'tile'), may hold values from 0.5 to 2
- momentum: float32 [3, 64, 128, 128], P(None, 'depth', 'tile'), may hold values from -4 to 4
- magnetic: float32 [3, 64, 128, 128], P(None, 'depth', 'tile'), may hold values from -4 to 4
- energy: float32 [64, 128, 128], P('depth', 'tile'), may hold values from 2 to 4
- shifts: int32 [24], replicated, may hold values from 0 to 55, as said below
- levels: int32 [24], replicated, may hold values from 0 to 63, as said below
Outputs:
- new_state: float32 [8, 64, 128, 128], P(None, 'depth', 'tile')
- intensity: float32 [48, 128, 128], P(None, 'tile', 'depth')
Inputs may be any that keep to these rules, and one draw needn't show every extreme that they name: shifts[k] = (1732 (levels[k] - levels[0]) + 1000) // 2000, the nearest whole column to tan(60 degrees) times the depth gap at half a column per level; the last is exactly 55. 24 distinct levels in ascending order, the first 0 and the last 63; each depth slab of 16 consecutive levels holds at most 8 of them, and some slab exactly 8.
All inputs are finite; a program needn't handle non-finite values.
Results may differ from a plain program's by a relative error of at most 0.000054.
Values sent between devices are 32-bit elements; how exact they have to be, the bound alone decides.
A program may use at most 64 MiB of HBM per device.

v0:
```python
import jax
import jax.numpy as jnp
from jax import lax
from jax.sharding import PartitionSpec as P

W = 48
GAMMA = 5.0 / 3.0
SECTION = 0.02
GRAVITY = 0.5
SIN_VIEW = 0.8660254037844386
COS_VIEW = 0.5
STRENGTH = 4.0
SPACING = 0.25


def shifted(block, axis, distance):
    devices = range(lax.axis_size(axis))
    route = [((i - distance) % len(devices), i) for i in devices]
    return lax.ppermute(block, axis, route)


def padded_2(cells, sides, width, closed):
    for axis, dim in sides:
        count = lax.axis_size(axis)
        ends = count if closed else count - 1
        head = lax.slice_in_dim(cells, 0, width, axis=dim)
        tail = lax.slice_in_dim(cells, cells.shape[dim] - width, cells.shape[dim], axis=dim)
        cells = jnp.concatenate(
            [
                lax.ppermute(tail, axis, [(i, (i + 1) % count) for i in range(ends)]),
                cells,
                lax.ppermute(head, axis, [((i + 1) % count, i) for i in range(ends)]),
            ],
            axis=dim,
        )
    return cells


def derive(padded, axis, count):

    def layer(offset):
        return lax.slice_in_dim(padded, offset, offset + count, axis=axis)

    return (
        45.0 * (layer(4) - layer(2)) - 9.0 * (layer(5) - layer(1)) + (layer(6) - layer(0))
    ) / 60.0


def flux(state, comp):
    rho = state[0]
    moment = state[1:4]
    field = state[4:7]
    energy = state[7]
    velocity = moment / rho
    field_sq = jnp.sum(field * field, axis=0)
    pressure = (GAMMA - 1.0) * (energy - 0.5 * jnp.sum(moment * velocity, axis=0) - 0.5 * field_sq)
    total = pressure + 0.5 * field_sq
    along = velocity[comp]
    normal = field[comp]
    flux_mom = (moment * along - field * normal).at[comp].add(total)
    flux_mag = along * field - normal * velocity
    flux_energy = (energy + total) * along - normal * jnp.sum(velocity * field, axis=0)
    return jnp.concatenate([moment[comp][None], flux_mom, flux_mag, flux_energy[None]], axis=0)


def tendency(along_x, along_y, along_z, state):
    depth_cells, width_cells, cross_cells = (state.shape[1], state.shape[2], state.shape[3])
    rate = -(
        derive(flux(along_x, 0), 2, width_cells)
        + derive(flux(along_y, 1), 3, cross_cells)
        + derive(flux(along_z, 2), 1, depth_cells)
    )
    rate = rate.at[3].add(GRAVITY * state[0])
    rate = rate.at[7].add(GRAVITY * state[3])
    return rate


def line_fields(new_state):
    dens = 0.5 + jax.nn.softplus(new_state[0])
    speed = (COS_VIEW * new_state[3] + SIN_VIEW * new_state[1]) / dens
    field_sq = jnp.sum(new_state[4:7] * new_state[4:7], axis=0)
    source = jax.nn.softplus(new_state[7] - 0.5 * field_sq) / dens
    return jnp.stack([dens, speed, source], axis=1)


def rows_mask(flags):
    return flags[:, None, None, None]


def shear(rows, row_shift, reach):
    cells = rows.shape[2]
    tiles_ahead = row_shift // cells
    offset = row_shift % cells

    def advance(turn, carry):
        piece, near, beyond = carry
        piece = shifted(piece, "tile", -1)
        near = jnp.where(rows_mask(tiles_ahead == turn), piece, near)
        beyond = jnp.where(rows_mask(tiles_ahead + 1 == turn), piece, beyond)
        return (piece, near, beyond)

    start_near = jnp.where(rows_mask(tiles_ahead == 0), rows, jnp.zeros_like(rows))
    carry = lax.fori_loop(1, reach + 2, advance, (rows, start_near, jnp.zeros_like(rows)))
    near = carry[1]
    beyond = carry[2]
    joined = jnp.concatenate([near, beyond], axis=2)
    target = jnp.arange(cells, dtype=jnp.int32)
    anchor = jnp.arange(2 * cells, dtype=jnp.int32)
    select = (anchor[None, None, :] == target[None, :, None] + offset[:, None, None]).astype(
        jnp.float32
    )
    return jnp.einsum("lcxa,lwx->lcwa", joined, select, precision=lax.Precision.HIGHEST)


def regroup(rows):
    return lax.all_to_all(rows, "depth", split_axis=3, concat_axis=0, tiled=True)


def emergent(columns):
    positions = columns.shape[0]
    flat = columns.reshape(positions, 3, -1)
    dens = flat[:, 0]
    speed = flat[:, 1]
    source = flat[:, 2]
    waves = (jnp.arange(W, dtype=jnp.float32) - 0.5 * (W - 1)) * SPACING
    gap = waves[:, None, None] - speed[None]
    dtau = 2.0 / positions * dens[None] * (1.0 + STRENGTH * jnp.exp(-gap * gap))
    order = jnp.arange(positions, dtype=jnp.int32)
    earlier = (order[None, :] < order[:, None]).astype(jnp.float32)
    above = jnp.einsum("kj,wjc->wkc", earlier, dtau, precision=lax.Precision.HIGHEST)
    inner = jnp.sum(source[None] * jnp.exp(-above) * (1.0 - jnp.exp(-dtau)), axis=1)
    total = inner + source[-1][None] * jnp.exp(-above[:, -1] - dtau[:, -1])
    return total.reshape((W,) + columns.shape[2:])


def per_device(density, momentum, magnetic, energy, shifts, levels):
    state = jnp.concatenate([density[None], momentum, magnetic, energy[None]], axis=0)
    count_vars, depth_cells, width_cells, cross_cells = state.shape
    depth_at = lax.axis_index("depth")
    slabs = lax.axis_size("depth")
    along_x = padded_2(state, (("tile", 2),), 3, True)
    padded = padded_2(state, (("depth", 1),), 3, False)
    rim_shape = (count_vars, 3, width_cells, cross_cells)
    head = jnp.where(depth_at == 0, jnp.broadcast_to(state[:, :1], rim_shape), padded[:, :3])
    tail = jnp.where(
        depth_at == slabs - 1,
        jnp.broadcast_to(state[:, -1:], rim_shape),
        padded[:, depth_cells + 3 :],
    )
    along_z = jnp.concatenate([head, state, tail], axis=1)
    along_y = jnp.pad(state, ((0, 0), (0, 0), (0, 0), (3, 3)), mode="wrap")
    new_state = state + SECTION * tendency(along_x, along_y, along_z, state)
    fields = line_fields(new_state)
    largest = (1732 * (depth_cells * slabs - 1) + 1000) // 2000
    reach = largest // width_cells
    lowest = depth_at * depth_cells
    local_level = lowest + jnp.arange(depth_cells, dtype=jnp.int32)
    match = local_level[:, None] == levels[None, :]
    level_shift = jnp.sum(jnp.where(match, shifts[None, :], 0), axis=1)
    columns = regroup(shear(fields, level_shift, reach))[levels]
    intensity = emergent(columns)
    return (new_state, intensity)


def solution(mesh):
    return jax.shard_map(
        per_device,
        mesh=mesh,
        in_specs=(
            P("depth", "tile", None),
            P(None, "depth", "tile", None),
            P(None, "depth", "tile", None),
            P("depth", "tile", None),
            P(),
            P(),
        ),
        out_specs=(P(None, "depth", "tile", None), P(None, "tile", "depth")),
        check_vma=False,
    )
```

profile of v0, /device:TPU:0, one launch (start us, length us, event | category | flops | bytes accessed | tf_op | source)
XLA Modules:
  0.0 125.3 jit_solution(16690774001178542910)
XLA Ops:
  0.6 1.3 %pad_maximum_fusion.4 = f32[8,16,16,128]{3,2,1,0:T(8,128)S(1)} fusion(f32[1,16,16,128]{3,2,1,0:T(8,128)} %bitcast.161, f32[3,16,16,128]{3,2,1,0:T(8,128)} %param.20, f32[3,16,16,128]{3,2,1,0:T(8,128)} %param.19, f32[1,16,16,128]{3,2,1,0:T(8,128)} %bitcast.147), kind=kLoop, calls=%fused_computation.76 | loop fusion | flops 786432 | bytes 2097152 | tf_op jit(solution)/shard_map/concatenate | solution.py:137
  1.9 0.8 fusion.81
  2.7 1.3 %collective-permute-start.4 = (f32[8,3,16,128]{3,2,1,0:T(8,128)}, f32[8,3,16,128]{3,2,1,0:T(8,128)}, u32[]{:S(2)}, u32[]{:S(2)}) collective-permute-start(f32[8,3,16,128]{3,2,1,0:T(8,128)} %get-tuple-element.273), channel_id=1, source_target_pairs={{1,0},{2,1},{3,2},{5,4},{6,5},{7,6},{9,8},{10,9},{11,10},{13,12},{... | collective-permute-start | bytes 589832 | tf_op jit(solution)/shard_map/ppermute | solution.py:32
  4.0 3.7 %collective-permute-start.3 = (f32[8,3,16,128]{3,2,1,0:T(8,128)}, f32[8,3,16,128]{3,2,1,0:T(8,128)}, u32[]{:S(2)}, u32[]{:S(2)}) collective-permute-start(f32[8,3,16,128]{3,2,1,0:T(8,128)} %get-tuple-element.272), channel_id=1, source_target_pairs={{0,1},{1,2},{2,3},{4,5},{5,6},{6,7},{8,9},{9,10},{10,11},{12,13},{... | collective-permute-start | bytes 589832 | tf_op jit(solution)/shard_map/ppermute | solution.py:30
  7.7 0.9 fusion.79
  8.7 6.0 %collective-permute-start.2 = (f32[8,16,3,128]{3,2,1,0:T(4,128)}, f32[8,16,3,128]{3,2,1,0:T(4,128)}, u32[]{:S(2)}, u32[]{:S(2)}) collective-permute-start(f32[8,16,3,128]{3,2,1,0:T(4,128)} %get-tuple-element.267), channel_id=1, source_target_pairs={{4,0},{8,4},{12,8},{16,12},{20,16},{24,20},{28,24},{0,28},{5,1},{9... | collective-permute-start | bytes 589832 | tf_op jit(solution)/shard_map/ppermute | solution.py:32
  14.7 0.7 slice_bitcast_fusion.6
  15.3 0.3 fusion.80
  15.7 0.6 copy-done
  16.3 0.1 copy-done.1
  16.5 1.1 maximum_bitcast_fusion
  17.6 2.2 %pad_maximum_fusion = f32[8,16,16,134]{3,2,1,0:T(8,128)} fusion(f32[8,16,16,3]{3,2,1,0:T(8,128)S(1)} %get-tuple-element.269, f32[1,16,16,128]{3,2,1,0:T(8,128)S(1)} %bitcast.163, f32[3,16,16,128]{3,2,1,0:T(8,128)S(1)} %copy-done.1, f32[3,16,16,128]{3,2,1,0:T(8,128)S(1)} %copy-done, f32[1,16,16,128]{3,2,1,0:T(8,128)S(1)} %bitcast.149, ...), kind=kLoop, calls=%fused_computation.23 | loop fusion | flops 1372160 | bytes 2195456 | tf_op jit(solution)/shard_map/jit(_pad)/concatenate | solution.py:151
  19.8 0.6 add_multiply_fusion
  20.4 3.5 %multiply_reduce_fusion.3 = (f32[16,16,134]{2,1,0:T(8,128)}, f32[16,16,134]{2,1,0:T(8,128)}, f32[16,16,134]{2,1,0:T(8,128)}, f32[3,16,16,134]{3,2,1,0:T(8,128)}) fusion(f32[8,16,16,134]{3,2,1,0:T(8,128)} %pad_maximum_fusion, f32[16,16,134]{2,1,0:T(8,128)} %get-tuple-element.251), kind=kLoop, calls=%fused_computation.84 | loop fusion | flops 617472 | bytes 1783808 | tf_op jit(solution)/shard_map/reduce_sum | solution.py:56
  23.9 1.7 %slice_bitcast_fusion = f32[16,16,134]{2,1,0:T(8,128)} fusion(f32[3,16,16,134]{3,2,1,0:T(8,128)} %get-tuple-element.243), kind=kLoop, calls=%fused_computation.116 | loop fusion | bytes 274432 | tf_op jit(solution)/shard_map/mul | solution.py:60
  25.6 0.2 select_reduce_fusion
  25.8 2.1 %multiply_subtract_fusion = (f32[3,16,16,134]{3,2,1,0:T(8,128)S(1)}, f32[3,16,16,134]{3,2,1,0:T(8,128)S(1)}) fusion(f32[3,16,16,134]{3,2,1,0:T(8,128)} %get-tuple-element.243, f32[8,16,16,134]{3,2,1,0:T(8,128)} %pad_maximum_fusion, f32[16,16,134]{2,1,0:T(8,128)} %bitcast.178, f32[16,16,134]{2,1,0:T(8,128)} %slice_bitcast_fusion), kind=kLoop, calls=%fused_computation.82 | loop fusion | flops 617472 | bytes 2332672 | tf_op jit(solution)/shard_map/sub | solution.py:61
  28.0 0.3 fusion.50
  28.3 0.7 copy-done.5
  29.0 1.1 fusion.51
  30.2 0.3 fusion.6
  30.5 0.5 copy-done.10
  31.0 0.9 broadcast_select_fusion.2
  32.1 0.1 multiply_reduce_fusion.9
  32.3 0.9 maximum_bitcast_fusion.1
  33.2 1.3 %pad_maximum_fusion.1 = f32[8,16,22,128]{3,2,1,0:T(8,128)S(1)} fusion(f32[8,16,3,128]{3,2,1,0:T(4,128)} %collective-permute-done.2, f32[1,16,16,128]{3,2,1,0:T(8,128)S(1)} %bitcast.169, f32[3,16,16,128]{3,2,1,0:T(8,128)S(1)} %copy-done.1, f32[3,16,16,128]{3,2,1,0:T(8,128)S(1)} %copy-done, f32[1,16,16,128]{3,2,1,0:T(8,128)S(1)} %bitcast.155, ...), kind=kLoop, calls=%fused_computation.37 | loop fusion | flops 1802240 | bytes 2883584 | tf_op jit(solution)/shard_map/concatenate | solution.py:28
  34.5 0.2 multiply_reduce_fusion.6
  34.7 0.1 multiply_subtract_fusion.4
  35.0 0.2 multiply_subtract_fusion.2
  35.2 0.9 fusion.53
  36.3 1.2 fusion.15
  37.5 1.6 %fusion.33 = f32[8,16,16,128]{3,2,1,0:T(8,128)S(1)} fusion(f32[8,22,16,128]{3,2,1,0:T(8,128)S(1)} %fusion.24, f32[8,16,16,134]{3,2,1,0:T(8,128)S(1)} %fusion.6, f32[8,16,22,128]{3,2,1,0:T(8,128)S(1)} %fusion.15), kind=kLoop, calls=%fused_computation.55 | loop fusion | flops 6553600 | bytes 19922944 | tf_op jit(solution)/shard_map/neg | solution.py:68
  39.2 0.1 multiply_add_fusion
  39.4 0.2 fusion.59
  39.7 0.6 copy-done.4
  40.3 53.6 %while.23 = (s32[]{:T(128)}, f32[16,3,16,128]{3,2,1,0:T(8,128)S(1)}, f32[16,3,16,128]{3,2,1,0:T(8,128)S(1)}, f32[16,3,16,128]{3,2,1,0:T(8,128)S(1)}, s32[16]{0:T(128)S(1)}, /*index=5*/s32[]{:T(128)}, s32[]{:T(128)}) while((s32[]{:T(128)}, f32[16,3,16,128]{3,2,1,0:T(8,128)S(1)}, f32[16,3,16,128]{3,2,1,0:T(8,128)S(1)}, ...), condition=%wide.region_12.13_spmd.clone, body=%wide.region_11.12_spmd.clone.sunk | while | flops 294963 | bytes 4325643 | solution.py:103
  40.3 4.8 %collective-permute-start = (f32[16,3,16,128]{3,2,1,0:T(8,128)S(1)}, f32[16,3,16,128]{3,2,1,0:T(8,128)S(1)}, u32[]{:S(2)}, u32[]{:S(2)}) collective-permute-start(f32[16,3,16,128]{3,2,1,0:T(8,128)S(1)} %get-tuple-element.331), channel_id=1, source_target_pairs={{4,0},{8,4},{12,8},{16,12},{20,16},{24,20},{28,24},{0,28},{5,1},{9... | collective-permute-start | bytes 1179656 | tf_op jit(solution)/shard_map/while/body/eval_jaxpr/ppermute | solution.py:19
  45.1 9.4 %collective-permute-done = f32[16,3,16,128]{3,2,1,0:T(8,128)S(1)} collective-permute-done((f32[16,3,16,128]{3,2,1,0:T(8,128)S(1)}, f32[16,3,16,128]{3,2,1,0:T(8,128)S(1)}, u32[]{:S(2)}, u32[]{:S(2)}) %collective-permute-start) | collective-permute-done | bytes 393248 | tf_op jit(solution)/shard_map/while/body/eval_jaxpr/ppermute | solution.py:19
  54.5 0.2 select_select_fusion.2
  54.7 5.2 %collective-permute-start = (f32[16,3,16,128]{3,2,1,0:T(8,128)S(1)}, f32[16,3,16,128]{3,2,1,0:T(8,128)S(1)}, u32[]{:S(2)}, u32[]{:S(2)}) collective-permute-start(f32[16,3,16,128]{3,2,1,0:T(8,128)S(1)} %get-tuple-element.331), channel_id=1, source_target_pairs={{4,0},{8,4},{12,8},{16,12},{20,16},{24,20},{28,24},{0,28},{5,1},{9... | collective-permute-start | bytes 1179656 | tf_op jit(solution)/shard_map/while/body/eval_jaxpr/ppermute | solution.py:19
  59.9 8.5 %collective-permute-done = f32[16,3,16,128]{3,2,1,0:T(8,128)S(1)} collective-permute-done((f32[16,3,16,128]{3,2,1,0:T(8,128)S(1)}, f32[16,3,16,128]{3,2,1,0:T(8,128)S(1)}, u32[]{:S(2)}, u32[]{:S(2)}) %collective-permute-start) | collective-permute-done | bytes 393248 | tf_op jit(solution)/shard_map/while/body/eval_jaxpr/ppermute | solution.py:19
  68.5 0.2 select_select_fusion.2
  68.7 5.2 %collective-permute-start = (f32[16,3,16,128]{3,2,1,0:T(8,128)S(1)}, f32[16,3,16,128]{3,2,1,0:T(8,128)S(1)}, u32[]{:S(2)}, u32[]{:S(2)}) collective-permute-start(f32[16,3,16,128]{3,2,1,0:T(8,128)S(1)} %get-tuple-element.331), channel_id=1, source_target_pairs={{4,0},{8,4},{12,8},{16,12},{20,16},{24,20},{28,24},{0,28},{5,1},{9... | collective-permute-start | bytes 1179656 | tf_op jit(solution)/shard_map/while/body/eval_jaxpr/ppermute | solution.py:19
  73.9 7.6 %collective-permute-done = f32[16,3,16,128]{3,2,1,0:T(8,128)S(1)} collective-permute-done((f32[16,3,16,128]{3,2,1,0:T(8,128)S(1)}, f32[16,3,16,128]{3,2,1,0:T(8,128)S(1)}, u32[]{:S(2)}, u32[]{:S(2)}) %collective-permute-start) | collective-permute-done | bytes 393248 | tf_op jit(solution)/shard_map/while/body/eval_jaxpr/ppermute | solution.py:19
  81.6 0.2 select_select_fusion.2
  81.7 5.2 %collective-permute-start = (f32[16,3,16,128]{3,2,1,0:T(8,128)S(1)}, f32[16,3,16,128]{3,2,1,0:T(8,128)S(1)}, u32[]{:S(2)}, u32[]{:S(2)}) collective-permute-start(f32[16,3,16,128]{3,2,1,0:T(8,128)S(1)} %get-tuple-element.331), channel_id=1, source_target_pairs={{4,0},{8,4},{12,8},{16,12},{20,16},{24,20},{28,24},{0,28},{5,1},{9... | collective-permute-start | bytes 1179656 | tf_op jit(solution)/shard_map/while/body/eval_jaxpr/ppermute | solution.py:19
  87.0 6.8 %collective-permute-done = f32[16,3,16,128]{3,2,1,0:T(8,128)S(1)} collective-permute-done((f32[16,3,16,128]{3,2,1,0:T(8,128)S(1)}, f32[16,3,16,128]{3,2,1,0:T(8,128)S(1)}, u32[]{:S(2)}, u32[]{:S(2)}) %collective-permute-start) | collective-permute-done | bytes 393248 | tf_op jit(solution)/shard_map/while/body/eval_jaxpr/ppermute | solution.py:19
  93.8 0.2 select_select_fusion.2
  94.0 1.2 convolution_bitcast_fusion.1
  95.2 2.1 %copy.37 = f32[16,3,16,128]{2,0,1,3:T(8,128)S(1)} copy(f32[16,3,16,128]{3,2,1,0:T(8,128)} %convolution_bitcast_fusion.1) | data formatting | bytes 786432 | tf_op jit(solution)/shard_map/lcxa,lwx->lcwa/transpose | solution.py:112
  97.2 1.8 %reshape.515 = f32[4,1,24576]{2,1,0:T(1,128)} reshape(f32[128,3,16,16]{3,2,1,0:T(8,128)S(1)} %bitcast.175) | data formatting | bytes 786432
  99.1 3.6 %all-to-all-start = ((f32[4,1,24576]{2,1,0:T(1,128)}), f32[4,1,24576]{2,1,0:T(1,128)S(1)}, u32[]{:S(2)}, u32[]{:S(2)}) async-start(f32[4,1,24576]{2,1,0:T(1,128)} %reshape.515), calls=%async_computation | async-start | bytes 786432 | tf_op jit(solution)/shard_map/all_to_all | solution.py:116
  102.8 7.2 %all-to-all-done = f32[4,1,24576]{2,1,0:T(1,128)S(1)} async-done(((f32[4,1,24576]{2,1,0:T(1,128)}), f32[4,1,24576]{2,1,0:T(1,128)S(1)}, u32[]{:S(2)}, u32[]{:S(2)}) %all-to-all-start) | async-done | bytes 393248 | tf_op jit(solution)/shard_map/all_to_all | solution.py:116
  109.9 0.5 broadcast.492
  110.4 1.8 %reduce.16 = f32[4,24576]{1,0:T(4,128)S(1)} reduce(f32[4,1,24576]{2,1,0:T(1,128)S(1)} %all-to-all-done, f32[]{:T(128)} %broadcast.492), dimensions={1}, to_apply=%all_to_all.13.reduce_sub_computation | reduce | bytes 786436 | tf_op jit(solution)/shard_map/all_to_all | solution.py:116
  112.2 1.1 reshape.516
  113.3 2.2 %copy.38 = f32[16,3,16,4,32]{4,2,1,0,3:T(8,128)} copy(f32[16,3,16,4,32]{2,0,1,4,3:T(8,128)S(1)} %bitcast.176) | data formatting | bytes 786432 | tf_op jit(solution)/shard_map/all_to_all | solution.py:116
  115.6 2.0 %gather_fusion = f32[24,3,16,32]{3,2,1,0:T(8,128)S(1)} fusion(f32[64,3,16,32]{3,2,1,0:T(8,128)} %bitcast.177, s32[1024]{0:T(1024)S(1)} %pad_clamp_fusion), kind=kCustom, calls=%fused_computation | custom fusion | bytes 295008 | tf_op jit(solution)/shard_map/gather | solution.py:160
  117.6 0.3 reshape.506
  118.0 4.4 %fusion.3 = (f32[48,24,512]{2,1,0:T(8,128)S(1)}, f32[48,512]{1,0:T(8,128)S(1)}, f32[48,24,512]{2,1,0:T(8,128)}) fusion(f32[24,512]{1,0:T(8,128)S(1)} %get-tuple-element.282, f32[48]{0:T(128)S(1)} %copy-done.13, f32[24,512]{1,0:T(8,128)S(1)} %get-tuple-element.283, f32[24,512]{1,0:T(8,128)S(1)} %bitcast.181), kind=kOutput, calls=%fused_computation.9 | convolution fusion | flops 180462144 | bytes 4964544 | tf_op jit(solution)/shard_map/kj,wjc->wkc/dot_general | solution.py:130
  122.4 0.1 reduce_sum.131
  122.6 1.6 %fusion.70 = f32[48,512]{1,0:T(8,128)S(1)} fusion(f32[48,24,512]{2,1,0:T(8,128)S(1)} %get-tuple-element.279, f32[48,24,512]{2,1,0:T(8,128)} %get-tuple-element.281), kind=kLoop, calls=%fused_computation.163 | loop fusion | flops 49152 | bytes 294912 | tf_op jit(solution)/shard_map/exp | solution.py:132
  124.1 0.1 exp.51
  124.4 0.9 copy.40
  (64 shorter events, 1.5 us)
Async XLA Ops:
  2.7 27.7 %collective-permute-start.4 = (f32[8,3,16,128]{3,2,1,0:T(8,128)}, f32[8,3,16,128]{3,2,1,0:T(8,128)}, u32[]{:S(2)}, u32[]{:S(2)}) collective-permute-start(f32[8,3,16,128]{3,2,1,0:T(8,128)} %get-tuple-element.273), channel_id=1, source_target_pairs={{1,0},{2,1},{3,2},{5,4},{6,5},{7,6},{9,8},{10,9},{11,10},{13,12},{... | collective-permute-start | bytes 589832 | tf_op jit(solution)/shard_map/ppermute | solution.py:32
  4.0 27.9 %collective-permute-start.3 = (f32[8,3,16,128]{3,2,1,0:T(8,128)}, f32[8,3,16,128]{3,2,1,0:T(8,128)}, u32[]{:S(2)}, u32[]{:S(2)}) collective-permute-start(f32[8,3,16,128]{3,2,1,0:T(8,128)} %get-tuple-element.272), channel_id=1, source_target_pairs={{0,1},{1,2},{2,3},{4,5},{5,6},{6,7},{8,9},{9,10},{10,11},{12,13},{... | collective-permute-start | bytes 589832 | tf_op jit(solution)/shard_map/ppermute | solution.py:30
  8.7 23.6 %collective-permute-start.2 = (f32[8,16,3,128]{3,2,1,0:T(4,128)}, f32[8,16,3,128]{3,2,1,0:T(4,128)}, u32[]{:S(2)}, u32[]{:S(2)}) collective-permute-start(f32[8,16,3,128]{3,2,1,0:T(4,128)} %get-tuple-element.267), channel_id=1, source_target_pairs={{4,0},{8,4},{12,8},{16,12},{20,16},{24,20},{28,24},{0,28},{5,1},{9... | collective-permute-start | bytes 589832 | tf_op jit(solution)/shard_map/ppermute | solution.py:32
  14.7 17.7 %collective-permute-start.1 = (f32[8,16,3,128]{3,2,1,0:T(4,128)}, f32[8,16,3,128]{3,2,1,0:T(4,128)}, u32[]{:S(2)}, u32[]{:S(2)}) collective-permute-start(f32[8,16,3,128]{3,2,1,0:T(4,128)} %get-tuple-element.266), channel_id=1, source_target_pairs={{0,4},{4,8},{8,12},{12,16},{16,20},{20,24},{24,28},{28,0},{1,5},{5... | collective-permute-start | bytes 589832 | tf_op jit(solution)/shard_map/ppermute | solution.py:30
  15.3 1.0 copy-start
  15.3 1.1 copy-start.1
  15.3 1.1 copy-start.2
  15.3 1.2 copy-start.3
  20.4 5.2 %copy-start.11 = (s32[24]{0:T(128)S(1)}, s32[24]{0:T(128)}, u32[]{:S(2)}) copy-start(s32[24]{0:T(128)} %param.22) | copy-start | bytes 292
  20.4 5.2 %copy-start.12 = (s32[24]{0:T(128)S(1)}, s32[24]{0:T(128)}, u32[]{:S(2)}) copy-start(s32[24]{0:T(128)} %param.23) | copy-start | bytes 292
  25.8 2.1 %copy-start.6 = (f32[16,16,134]{2,1,0:T(8,128)S(1)}, f32[16,16,134]{2,1,0:T(8,128)}, u32[]{:S(2)}) copy-start(f32[16,16,134]{2,1,0:T(8,128)} %get-tuple-element.217) | copy-start | bytes 411652
  25.8 2.2 %copy-start.7 = (f32[16,16,134]{2,1,0:T(8,128)S(1)}, f32[16,16,134]{2,1,0:T(8,128)}, u32[]{:S(2)}) copy-start(f32[16,16,134]{2,1,0:T(8,128)} %get-tuple-element.221) | copy-start | bytes 411652
  28.0 1.0 copy-start.5
  28.0 1.0 copy-start.8
  30.1 0.8 copy-start.10
  30.1 1.8 %copy-start.9 = (f32[8,16,128]{2,1,0:T(8,128)S(1)}, f32[8,16,128]{2,1,0:T(8,128)}, u32[]{:S(2)}) copy-start(f32[8,16,128]{2,1,0:T(8,128)} %get-tuple-element.270) | copy-start | bytes 196612
  39.3 1.0 copy-start.4
  40.3 14.1 %collective-permute-start = (f32[16,3,16,128]{3,2,1,0:T(8,128)S(1)}, f32[16,3,16,128]{3,2,1,0:T(8,128)S(1)}, u32[]{:S(2)}, u32[]{:S(2)}) collective-permute-start(f32[16,3,16,128]{3,2,1,0:T(8,128)S(1)} %get-tuple-element.331), channel_id=1, source_target_pairs={{4,0},{8,4},{12,8},{16,12},{20,16},{24,20},{28,24},{0,28},{5,1},{9... | collective-permute-start | bytes 1179656 | tf_op jit(solution)/shard_map/while/body/eval_jaxpr/ppermute | solution.py:19
  54.7 13.7 %collective-permute-start = (f32[16,3,16,128]{3,2,1,0:T(8,128)S(1)}, f32[16,3,16,128]{3,2,1,0:T(8,128)S(1)}, u32[]{:S(2)}, u32[]{:S(2)}) collective-permute-start(f32[16,3,16,128]{3,2,1,0:T(8,128)S(1)} %get-tuple-element.331), channel_id=1, source_target_pairs={{4,0},{8,4},{12,8},{16,12},{20,16},{24,20},{28,24},{0,28},{5,1},{9... | collective-permute-start | bytes 1179656 | tf_op jit(solution)/shard_map/while/body/eval_jaxpr/ppermute | solution.py:19
  68.7 12.9 %collective-permute-start = (f32[16,3,16,128]{3,2,1,0:T(8,128)S(1)}, f32[16,3,16,128]{3,2,1,0:T(8,128)S(1)}, u32[]{:S(2)}, u32[]{:S(2)}) collective-permute-start(f32[16,3,16,128]{3,2,1,0:T(8,128)S(1)} %get-tuple-element.331), channel_id=1, source_target_pairs={{4,0},{8,4},{12,8},{16,12},{20,16},{24,20},{28,24},{0,28},{5,1},{9... | collective-permute-start | bytes 1179656 | tf_op jit(solution)/shard_map/while/body/eval_jaxpr/ppermute | solution.py:19
  81.7 12.0 %collective-permute-start = (f32[16,3,16,128]{3,2,1,0:T(8,128)S(1)}, f32[16,3,16,128]{3,2,1,0:T(8,128)S(1)}, u32[]{:S(2)}, u32[]{:S(2)}) collective-permute-start(f32[16,3,16,128]{3,2,1,0:T(8,128)S(1)} %get-tuple-element.331), channel_id=1, source_target_pairs={{4,0},{8,4},{12,8},{16,12},{20,16},{24,20},{28,24},{0,28},{5,1},{9... | collective-permute-start | bytes 1179656 | tf_op jit(solution)/shard_map/while/body/eval_jaxpr/ppermute | solution.py:19
  99.1 10.8 %all-to-all-start = ((f32[4,1,24576]{2,1,0:T(1,128)}), f32[4,1,24576]{2,1,0:T(1,128)S(1)}, u32[]{:S(2)}, u32[]{:S(2)}) async-start(f32[4,1,24576]{2,1,0:T(1,128)} %reshape.515), calls=%async_computation | async-start | bytes 786432 | tf_op jit(solution)/shard_map/all_to_all | solution.py:116
  115.6 2.4 %copy-start.13 = (f32[48]{0:T(128)S(1)}, f32[48]{0:T(128)}, u32[]{:S(2)}) copy-start(f32[48]{0:T(128)} %add_multiply_fusion) | copy-start | bytes 580
where the time goes:
time: 126 us; the launch traced here: 125 us
  waiting for transfers between devices  39.5 us (31%)
  starting transfers between devices  35.1 us (28%)
  other arithmetic  25.2 us (20%)
  local copies, waits for them, and re-layouts  18.8 us (15%)
  matrix products  5.57 us (4%)
    ppermute x4, waiting for transfers between devices, shifted(): return lax.ppermute(block, axis, route)  32.3 us
    ppermute x4, starting transfers between devices, shifted(): return lax.ppermute(block, axis, route)  20.5 us
    ppermute x2, starting transfers between devices, padded_2(): lax.ppermute(head, axis, [((i + 1) % count, i) for i in range(ends)])  7.28 us
    all_to_all x1, waiting for transfers between devices, regroup(): lax.all_to_all(rows, 'depth', split_axis=3, concat_axis=0, tiled=True)  7.17 us
    unnamed x35, local copies, waits for them, and re-layouts  6.68 us
    dot_general x1, matrix products, emergent(): jnp.einsum('kj,wjc->wkc', earlier, dtau, precision=lax.Precision.HIGHEST)  4.39 us
    reduce_sum x3, other arithmetic, flux(): jnp.sum(moment * velocity, axis=0)  3.84 us
    ppermute x2, starting transfers between devices, padded_2(): lax.ppermute(tail, axis, [(i, (i + 1) % count) for i in range(ends)])  3.72 us
  transfers between devices with their start and end apart: 9, of which 5 were waited for; matrix products, arithmetic and copies ran while one was open for 13% of the time, Pallas kernels for 0%

commit v1 on v0

--- a/solution.py
+++ b/solution.py
@@ -113,7 +113,10 @@
 
 
 def regroup(rows):
-    return lax.all_to_all(rows, "depth", split_axis=3, concat_axis=0, tiled=True)
+    return jnp.concatenate(
+        lax.all_to_all(jnp.stack(jnp.split(rows, lax.axis_size("depth"), axis=3)), "depth", 0, 0),
+        axis=0,
+    )
 
 
 def emergent(columns):

time: 126 us -> 118 us (0.937)
  local copies, waits for them, and re-layouts: 18.8 us -> 12.3 us
    all_to_all x2 -> x1, local copies, waits for them, and re-layouts: 2.75 us -> 0.51 us  [regroup(): lax.all_to_all(jnp.stack(jnp.split(rows, lax.axis_size('depth'), axis=3))...]
    transpose x1 -> x0, local copies, waits for them, and re-layouts: 2.06 us -> none  [shear(): jnp.einsum('lcxa,lwx->lcwa', joined, select, precision=lax.Precision.HIGH...]
    gather x1, local copies, waits for them, and re-layouts: 1.99 us -> 0.59 us  [per_device(): columns = regroup(shear(fields, level_shift, reach))[levels]]
  transfers between devices with their start and end apart: 9 -> 9, of which waited for: 5 -> 5; matrix products, arithmetic and copies ran while one was open for 13% -> 12% of each run, Pallas kernels for 0% -> 0%
where the time goes in v1:
time: 118 us; the launch traced here: 117 us
  waiting for transfers between devices  39.5 us (33%)
  starting transfers between devices  35.1 us (30%)
  other arithmetic  24 us (20%)
  local copies, waits for them, and re-layouts  12.3 us (10%)
  matrix products  4.83 us (4%)
    ppermute x4, waiting for transfers between devices, shifted(): return lax.ppermute(block, axis, route)  32.3 us
    ppermute x4, starting transfers between devices, shifted(): return lax.ppermute(block, axis, route)  20.5 us
    ppermute x2, starting transfers between devices, padded_2(): lax.ppermute(head, axis, [((i + 1) % count, i) for i in range(ends)])  7.28 us
    all_to_all x1, waiting for transfers between devices, regroup(): lax.all_to_all(jnp.stack(jnp.split(rows, lax.axis_size('depth'), axis=3))...  7.17 us
    unnamed x35, local copies, waits for them, and re-layouts  6.55 us
    dot_general x1, matrix products, emergent(): jnp.einsum('kj,wjc->wkc', earlier, dtau, precision=lax.Precision.HIGHEST)  4.39 us
    ppermute x2, starting transfers between devices, padded_2(): lax.ppermute(tail, axis, [(i, (i + 1) % count) for i in range(ends)])  3.72 us
    all_to_all x1, starting transfers between devices, regroup(): lax.all_to_all(jnp.stack(jnp.split(rows, lax.axis_size('depth'), axis=3))...  3.64 us
  transfers between devices with their start and end apart: 9, of which 5 were waited for; matrix products, arithmetic and copies ran while one was open for 12% of the time, Pallas kernels for 0%

profile of v1, /device:TPU:0, one launch (start us, length us, event | category | flops | bytes accessed | tf_op | source)
XLA Modules:
  0.0 116.9 jit_solution(11248257557321033254)
XLA Ops:
  0.6 1.3 %pad_maximum_fusion.5 = f32[8,16,16,128]{3,2,1,0:T(8,128)S(1)} fusion(f32[1,16,16,128]{3,2,1,0:T(8,128)} %bitcast.164, f32[3,16,16,128]{3,2,1,0:T(8,128)} %param.20, f32[3,16,16,128]{3,2,1,0:T(8,128)} %param.19, f32[1,16,16,128]{3,2,1,0:T(8,128)} %bitcast.150), kind=kLoop, calls=%fused_computation.77 | loop fusion | flops 786432 | bytes 2097152 | tf_op jit(solution)/shard_map/concatenate | solution.py:140
  1.9 0.8 fusion.81
  2.7 1.3 %collective-permute-start.4 = (f32[8,3,16,128]{3,2,1,0:T(8,128)}, f32[8,3,16,128]{3,2,1,0:T(8,128)}, u32[]{:S(2)}, u32[]{:S(2)}) collective-permute-start(f32[8,3,16,128]{3,2,1,0:T(8,128)} %get-tuple-element.259), channel_id=1, source_target_pairs={{1,0},{2,1},{3,2},{5,4},{6,5},{7,6},{9,8},{10,9},{11,10},{13,12},{... | collective-permute-start | bytes 589832 | tf_op jit(solution)/shard_map/ppermute | solution.py:32
  4.0 3.7 %collective-permute-start.3 = (f32[8,3,16,128]{3,2,1,0:T(8,128)}, f32[8,3,16,128]{3,2,1,0:T(8,128)}, u32[]{:S(2)}, u32[]{:S(2)}) collective-permute-start(f32[8,3,16,128]{3,2,1,0:T(8,128)} %get-tuple-element.258), channel_id=1, source_target_pairs={{0,1},{1,2},{2,3},{4,5},{5,6},{6,7},{8,9},{9,10},{10,11},{12,13},{... | collective-permute-start | bytes 589832 | tf_op jit(solution)/shard_map/ppermute | solution.py:30
  7.7 0.9 fusion.79
  8.6 6.0 %collective-permute-start.2 = (f32[8,16,3,128]{3,2,1,0:T(4,128)}, f32[8,16,3,128]{3,2,1,0:T(4,128)}, u32[]{:S(2)}, u32[]{:S(2)}) collective-permute-start(f32[8,16,3,128]{3,2,1,0:T(4,128)} %get-tuple-element.253), channel_id=1, source_target_pairs={{4,0},{8,4},{12,8},{16,12},{20,16},{24,20},{28,24},{0,28},{5,1},{9... | collective-permute-start | bytes 589832 | tf_op jit(solution)/shard_map/ppermute | solution.py:32
  14.7 0.7 slice_bitcast_fusion.10
  15.3 0.3 fusion.80
  15.7 0.6 copy-done
  16.5 1.1 maximum_bitcast_fusion
  17.6 2.2 %pad_maximum_fusion = f32[8,16,16,134]{3,2,1,0:T(8,128)} fusion(f32[8,16,16,3]{3,2,1,0:T(8,128)S(1)} %get-tuple-element.255, f32[1,16,16,128]{3,2,1,0:T(8,128)S(1)} %bitcast.166, f32[3,16,16,128]{3,2,1,0:T(8,128)S(1)} %copy-done.1, f32[3,16,16,128]{3,2,1,0:T(8,128)S(1)} %copy-done, f32[1,16,16,128]{3,2,1,0:T(8,128)S(1)} %bitcast.152, ...), kind=kLoop, calls=%fused_computation.23 | loop fusion | flops 1372160 | bytes 2195456 | tf_op jit(solution)/shard_map/jit(_pad)/concatenate | solution.py:154
  19.8 2.7 %multiply_reduce_fusion.3 = (f32[16,16,134]{2,1,0:T(8,128)}, f32[16,16,134]{2,1,0:T(8,128)}, f32[16,16,134]{2,1,0:T(8,128)}, f32[3,16,16,134]{3,2,1,0:T(8,128)S(1)}) fusion(f32[8,16,16,134]{3,2,1,0:T(8,128)} %pad_maximum_fusion, f32[16,16,134]{2,1,0:T(8,128)} %get-tuple-element.237), kind=kLoop, calls=%fused_computation.85 | loop fusion | flops 617472 | bytes 1783808 | tf_op jit(solution)/shard_map/reduce_sum | solution.py:56
  22.5 0.9 copy-done.4
  23.4 0.7 slice_bitcast_fusion.4
  24.1 0.2 select_reduce_fusion
  24.4 2.1 %multiply_subtract_fusion = (f32[3,16,16,134]{3,2,1,0:T(8,128)S(1)}, f32[3,16,16,134]{3,2,1,0:T(8,128)S(1)}) fusion(f32[3,16,16,134]{3,2,1,0:T(8,128)} %copy-done.4, f32[8,16,16,134]{3,2,1,0:T(8,128)} %pad_maximum_fusion, f32[16,16,134]{2,1,0:T(8,128)} %bitcast.179, f32[16,16,134]{2,1,0:T(8,128)} %slice_bitcast_fusion.4), kind=kLoop, calls=%fused_computation.83 | loop fusion | flops 617472 | bytes 2332672 | tf_op jit(solution)/shard_map/sub | solution.py:61
  26.5 0.3 fusion.50
  26.8 0.7 copy-done.6
  27.6 1.1 fusion.51
  28.7 0.3 fusion.6
  29.0 0.5 copy-done.11
  29.5 0.9 broadcast_select_fusion.2
  30.6 0.1 pad_maximum_fusion.4
  30.7 0.1 multiply_reduce_fusion.9
  30.9 0.9 maximum_bitcast_fusion.1
  31.8 1.3 %pad_maximum_fusion.1 = f32[8,16,22,128]{3,2,1,0:T(8,128)S(1)} fusion(f32[8,16,3,128]{3,2,1,0:T(4,128)} %collective-permute-done.2, f32[1,16,16,128]{3,2,1,0:T(8,128)S(1)} %bitcast.172, f32[3,16,16,128]{3,2,1,0:T(8,128)S(1)} %copy-done.1, f32[3,16,16,128]{3,2,1,0:T(8,128)S(1)} %copy-done, f32[1,16,16,128]{3,2,1,0:T(8,128)S(1)} %bitcast.158, ...), kind=kLoop, calls=%fused_computation.37 | loop fusion | flops 1802240 | bytes 2883584 | tf_op jit(solution)/shard_map/concatenate | solution.py:28
  33.0 0.2 multiply_reduce_fusion.6
  33.2 0.1 multiply_subtract_fusion.4
  33.6 0.2 multiply_subtract_fusion.2
  33.8 0.9 fusion.53
  34.9 1.2 %fusion.15 = f32[8,16,22,128]{3,2,1,0:T(8,128)S(1)} fusion(f32[8,16,3,128]{3,2,1,0:T(4,128)} %collective-permute-done.2, f32[8,16,3,128]{3,2,1,0:T(4,128)} %collective-permute-done.1, f32[1,16,16,128]{3,2,1,0:T(8,128)S(1)} %bitcast.176, f32[3,16,16,128]{3,2,1,0:T(8,128)S(1)} %copy-done.1, f32[3,16,16,128]{3,2,1,0:T(8,128)S(1)} %copy-done, ...), kind=kLoop, calls=%fused_computation.28 | loop fusion | flops 5046272 | bytes 4145152 | tf_op jit(solution)/shard_map/concatenate | solution.py:63
  36.1 1.6 %fusion.33 = f32[8,16,16,128]{3,2,1,0:T(8,128)S(1)} fusion(f32[8,22,16,128]{3,2,1,0:T(8,128)S(1)} %fusion.24, f32[8,16,16,134]{3,2,1,0:T(8,128)S(1)} %fusion.6, f32[8,16,22,128]{3,2,1,0:T(8,128)S(1)} %fusion.15), kind=kLoop, calls=%fused_computation.56 | loop fusion | flops 6553600 | bytes 19922944 | tf_op jit(solution)/shard_map/neg | solution.py:68
  37.7 0.1 multiply_add_fusion
  37.9 0.2 fusion.59
  38.3 0.6 copy-done.5
  38.9 53.6 %while.23 = (s32[]{:T(128)}, f32[16,3,16,128]{3,2,1,0:T(8,128)S(1)}, f32[16,3,16,128]{3,2,1,0:T(8,128)S(1)}, f32[16,3,16,128]{3,2,1,0:T(8,128)S(1)}, s32[16]{0:T(128)S(1)}, /*index=5*/s32[]{:T(128)}, s32[]{:T(128)}) while((s32[]{:T(128)}, f32[16,3,16,128]{3,2,1,0:T(8,128)S(1)}, f32[16,3,16,128]{3,2,1,0:T(8,128)S(1)}, ...), condition=%wide.region_12.13_spmd.clone, body=%wide.region_11.12_spmd.clone.sunk | while | flops 294963 | bytes 4325643 | solution.py:103
  38.9 4.8 %collective-permute-start = (f32[16,3,16,128]{3,2,1,0:T(8,128)S(1)}, f32[16,3,16,128]{3,2,1,0:T(8,128)S(1)}, u32[]{:S(2)}, u32[]{:S(2)}) collective-permute-start(f32[16,3,16,128]{3,2,1,0:T(8,128)S(1)} %get-tuple-element.321), channel_id=1, source_target_pairs={{4,0},{8,4},{12,8},{16,12},{20,16},{24,20},{28,24},{0,28},{5,1},{9... | collective-permute-start | bytes 1179656 | tf_op jit(solution)/shard_map/while/body/eval_jaxpr/ppermute | solution.py:19
  43.7 9.4 %collective-permute-done = f32[16,3,16,128]{3,2,1,0:T(8,128)S(1)} collective-permute-done((f32[16,3,16,128]{3,2,1,0:T(8,128)S(1)}, f32[16,3,16,128]{3,2,1,0:T(8,128)S(1)}, u32[]{:S(2)}, u32[]{:S(2)}) %collective-permute-start) | collective-permute-done | bytes 393248 | tf_op jit(solution)/shard_map/while/body/eval_jaxpr/ppermute | solution.py:19
  53.1 0.2 select_select_fusion.2
  53.3 5.2 %collective-permute-start = (f32[16,3,16,128]{3,2,1,0:T(8,128)S(1)}, f32[16,3,16,128]{3,2,1,0:T(8,128)S(1)}, u32[]{:S(2)}, u32[]{:S(2)}) collective-permute-start(f32[16,3,16,128]{3,2,1,0:T(8,128)S(1)} %get-tuple-element.321), channel_id=1, source_target_pairs={{4,0},{8,4},{12,8},{16,12},{20,16},{24,20},{28,24},{0,28},{5,1},{9... | collective-permute-start | bytes 1179656 | tf_op jit(solution)/shard_map/while/body/eval_jaxpr/ppermute | solution.py:19
  58.5 8.5 %collective-permute-done = f32[16,3,16,128]{3,2,1,0:T(8,128)S(1)} collective-permute-done((f32[16,3,16,128]{3,2,1,0:T(8,128)S(1)}, f32[16,3,16,128]{3,2,1,0:T(8,128)S(1)}, u32[]{:S(2)}, u32[]{:S(2)}) %collective-permute-start) | collective-permute-done | bytes 393248 | tf_op jit(solution)/shard_map/while/body/eval_jaxpr/ppermute | solution.py:19
  67.0 0.2 select_select_fusion.2
  67.2 5.2 %collective-permute-start = (f32[16,3,16,128]{3,2,1,0:T(8,128)S(1)}, f32[16,3,16,128]{3,2,1,0:T(8,128)S(1)}, u32[]{:S(2)}, u32[]{:S(2)}) collective-permute-start(f32[16,3,16,128]{3,2,1,0:T(8,128)S(1)} %get-tuple-element.321), channel_id=1, source_target_pairs={{4,0},{8,4},{12,8},{16,12},{20,16},{24,20},{28,24},{0,28},{5,1},{9... | collective-permute-start | bytes 1179656 | tf_op jit(solution)/shard_map/while/body/eval_jaxpr/ppermute | solution.py:19
  72.5 7.6 %collective-permute-done = f32[16,3,16,128]{3,2,1,0:T(8,128)S(1)} collective-permute-done((f32[16,3,16,128]{3,2,1,0:T(8,128)S(1)}, f32[16,3,16,128]{3,2,1,0:T(8,128)S(1)}, u32[]{:S(2)}, u32[]{:S(2)}) %collective-permute-start) | collective-permute-done | bytes 393248 | tf_op jit(solution)/shard_map/while/body/eval_jaxpr/ppermute | solution.py:19
  80.1 0.2 select_select_fusion.2
  80.3 5.2 %collective-permute-start = (f32[16,3,16,128]{3,2,1,0:T(8,128)S(1)}, f32[16,3,16,128]{3,2,1,0:T(8,128)S(1)}, u32[]{:S(2)}, u32[]{:S(2)}) collective-permute-start(f32[16,3,16,128]{3,2,1,0:T(8,128)S(1)} %get-tuple-element.321), channel_id=1, source_target_pairs={{4,0},{8,4},{12,8},{16,12},{20,16},{24,20},{28,24},{0,28},{5,1},{9... | collective-permute-start | bytes 1179656 | tf_op jit(solution)/shard_map/while/body/eval_jaxpr/ppermute | solution.py:19
  85.5 6.8 %collective-permute-done = f32[16,3,16,128]{3,2,1,0:T(8,128)S(1)} collective-permute-done((f32[16,3,16,128]{3,2,1,0:T(8,128)S(1)}, f32[16,3,16,128]{3,2,1,0:T(8,128)S(1)}, u32[]{:S(2)}, u32[]{:S(2)}) %collective-permute-start) | collective-permute-done | bytes 393248 | tf_op jit(solution)/shard_map/while/body/eval_jaxpr/ppermute | solution.py:19
  92.4 0.2 select_select_fusion.2
  92.5 0.4 convolution_bitcast_fusion.1
  93.0 0.4 slice_bitcast_fusion.3
  93.4 0.1 pad_maximum_fusion.2
  93.5 1.4 %reshape.519 = f32[4,1,24576]{2,1,0:T(1,128)} reshape(f32[4,16,3,16,32]{4,3,2,1,0:T(8,128)S(1)} %pad_maximum_fusion.2) | data formatting | bytes 786432
  95.0 3.6 %all-to-all-start = ((f32[4,1,24576]{2,1,0:T(1,128)}), f32[4,1,24576]{2,1,0:T(1,128)S(1)}, u32[]{:S(2)}, u32[]{:S(2)}) async-start(f32[4,1,24576]{2,1,0:T(1,128)} %reshape.519), calls=%async_computation | async-start | bytes 786432 | tf_op jit(solution)/shard_map/all_to_all | solution.py:117
  98.6 7.2 %all-to-all-done = f32[4,1,24576]{2,1,0:T(1,128)S(1)} async-done(((f32[4,1,24576]{2,1,0:T(1,128)}), f32[4,1,24576]{2,1,0:T(1,128)S(1)}, u32[]{:S(2)}, u32[]{:S(2)}) %all-to-all-start) | async-done | bytes 393248 | tf_op jit(solution)/shard_map/all_to_all | solution.py:117
  105.8 0.5 broadcast.492
  106.3 1.8 %reduce.16 = f32[4,24576]{1,0:T(4,128)S(1)} reduce(f32[4,1,24576]{2,1,0:T(1,128)S(1)} %all-to-all-done, f32[]{:T(128)} %broadcast.492), dimensions={1}, to_apply=%all_to_all.3.reduce_sub_computation | reduce | bytes 786436 | tf_op jit(solution)/shard_map/all_to_all | solution.py:117
  108.1 0.5 reshape.520
  108.6 0.6 gather_fusion
  109.2 0.3 reshape.510
  109.6 4.4 %fusion.3 = (f32[48,24,512]{2,1,0:T(8,128)S(1)}, f32[48,512]{1,0:T(8,128)S(1)}, f32[48,24,512]{2,1,0:T(8,128)}) fusion(f32[24,512]{1,0:T(8,128)S(1)} %get-tuple-element.272, f32[48]{0:T(128)S(1)} %add_multiply_fusion, f32[24,512]{1,0:T(8,128)S(1)} %get-tuple-element.273, f32[24,512]{1,0:T(8,128)S(1)} %bitcast.182), kind=kOutput, calls=%fused_computation.9 | convolution fusion | flops 180462144 | bytes 4964544 | tf_op jit(solution)/shard_map/kj,wjc->wkc/dot_general | solution.py:133
  114.0 0.1 reduce_sum.131
  114.2 1.6 %fusion.70 = f32[48,512]{1,0:T(8,128)S(1)} fusion(f32[48,24,512]{2,1,0:T(8,128)S(1)} %get-tuple-element.269, f32[48,24,512]{2,1,0:T(8,128)} %get-tuple-element.271), kind=kLoop, calls=%fused_computation.168 | loop fusion | flops 49152 | bytes 294912 | tf_op jit(solution)/shard_map/exp | solution.py:135
  115.7 0.1 exp.51
  116.0 0.9 copy.24
  (64 shorter events, 1.6 us)
Async XLA Ops:
  2.7 26.3 %collective-permute-start.4 = (f32[8,3,16,128]{3,2,1,0:T(8,128)}, f32[8,3,16,128]{3,2,1,0:T(8,128)}, u32[]{:S(2)}, u32[]{:S(2)}) collective-permute-start(f32[8,3,16,128]{3,2,1,0:T(8,128)} %get-tuple-element.259), channel_id=1, source_target_pairs={{1,0},{2,1},{3,2},{5,4},{6,5},{7,6},{9,8},{10,9},{11,10},{13,12},{... | collective-permute-start | bytes 589832 | tf_op jit(solution)/shard_map/ppermute | solution.py:32
  4.0 26.5 %collective-permute-start.3 = (f32[8,3,16,128]{3,2,1,0:T(8,128)}, f32[8,3,16,128]{3,2,1,0:T(8,128)}, u32[]{:S(2)}, u32[]{:S(2)}) collective-permute-start(f32[8,3,16,128]{3,2,1,0:T(8,128)} %get-tuple-element.258), channel_id=1, source_target_pairs={{0,1},{1,2},{2,3},{4,5},{5,6},{6,7},{8,9},{9,10},{10,11},{12,13},{... | collective-permute-start | bytes 589832 | tf_op jit(solution)/shard_map/ppermute | solution.py:30
  8.6 22.2 %collective-permute-start.2 = (f32[8,16,3,128]{3,2,1,0:T(4,128)}, f32[8,16,3,128]{3,2,1,0:T(4,128)}, u32[]{:S(2)}, u32[]{:S(2)}) collective-permute-start(f32[8,16,3,128]{3,2,1,0:T(4,128)} %get-tuple-element.253), channel_id=1, source_target_pairs={{4,0},{8,4},{12,8},{16,12},{20,16},{24,20},{28,24},{0,28},{5,1},{9... | collective-permute-start | bytes 589832 | tf_op jit(solution)/shard_map/ppermute | solution.py:32
  14.7 16.2 %collective-permute-start.1 = (f32[8,16,3,128]{3,2,1,0:T(4,128)}, f32[8,16,3,128]{3,2,1,0:T(4,128)}, u32[]{:S(2)}, u32[]{:S(2)}) collective-permute-start(f32[8,16,3,128]{3,2,1,0:T(4,128)} %get-tuple-element.252), channel_id=1, source_target_pairs={{0,4},{4,8},{8,12},{12,16},{16,20},{20,24},{24,28},{28,0},{1,5},{5... | collective-permute-start | bytes 589832 | tf_op jit(solution)/shard_map/ppermute | solution.py:30
  15.3 1.0 copy-start
  15.3 1.1 copy-start.1
  15.3 1.1 copy-start.2
  15.3 1.2 %copy-start.3 = (f32[16,16,128]{2,1,0:T(8,128)S(1)}, f32[16,16,128]{2,1,0:T(8,128)}, u32[]{:S(2)}) copy-start(f32[16,16,128]{2,1,0:T(8,128)} %param.21) | copy-start | bytes 393220
  19.8 4.3 %copy-start.12 = (s32[24]{0:T(128)S(1)}, s32[24]{0:T(128)}, u32[]{:S(2)}) copy-start(s32[24]{0:T(128)} %param.22) | copy-start | bytes 292
  19.8 4.3 %copy-start.13 = (s32[24]{0:T(128)S(1)}, s32[24]{0:T(128)}, u32[]{:S(2)}) copy-start(s32[24]{0:T(128)} %param.23) | copy-start | bytes 292
  22.5 0.9 copy-start.4
  24.4 2.1 %copy-start.7 = (f32[16,16,134]{2,1,0:T(8,128)S(1)}, f32[16,16,134]{2,1,0:T(8,128)}, u32[]{:S(2)}) copy-start(f32[16,16,134]{2,1,0:T(8,128)} %get-tuple-element.203) | copy-start | bytes 411652
  24.4 2.2 %copy-start.8 = (f32[16,16,134]{2,1,0:T(8,128)S(1)}, f32[16,16,134]{2,1,0:T(8,128)}, u32[]{:S(2)}) copy-start(f32[16,16,134]{2,1,0:T(8,128)} %get-tuple-element.207) | copy-start | bytes 411652
  26.5 1.0 copy-start.6
  26.5 1.0 copy-start.9
  28.7 0.8 copy-start.11
  28.7 1.8 %copy-start.10 = (f32[8,16,128]{2,1,0:T(8,128)S(1)}, f32[8,16,128]{2,1,0:T(8,128)}, u32[]{:S(2)}) copy-start(f32[8,16,128]{2,1,0:T(8,128)} %get-tuple-element.256) | copy-start | bytes 196612
  37.9 1.0 copy-start.5
  38.9 14.1 %collective-permute-start = (f32[16,3,16,128]{3,2,1,0:T(8,128)S(1)}, f32[16,3,16,128]{3,2,1,0:T(8,128)S(1)}, u32[]{:S(2)}, u32[]{:S(2)}) collective-permute-start(f32[16,3,16,128]{3,2,1,0:T(8,128)S(1)} %get-tuple-element.321), channel_id=1, source_target_pairs={{4,0},{8,4},{12,8},{16,12},{20,16},{24,20},{28,24},{0,28},{5,1},{9... | collective-permute-start | bytes 1179656 | tf_op jit(solution)/shard_map/while/body/eval_jaxpr/ppermute | solution.py:19
  53.3 13.7 %collective-permute-start = (f32[16,3,16,128]{3,2,1,0:T(8,128)S(1)}, f32[16,3,16,128]{3,2,1,0:T(8,128)S(1)}, u32[]{:S(2)}, u32[]{:S(2)}) collective-permute-start(f32[16,3,16,128]{3,2,1,0:T(8,128)S(1)} %get-tuple-element.321), channel_id=1, source_target_pairs={{4,0},{8,4},{12,8},{16,12},{20,16},{24,20},{28,24},{0,28},{5,1},{9... | collective-permute-start | bytes 1179656 | tf_op jit(solution)/shard_map/while/body/eval_jaxpr/ppermute | solution.py:19
  67.2 12.9 %collective-permute-start = (f32[16,3,16,128]{3,2,1,0:T(8,128)S(1)}, f32[16,3,16,128]{3,2,1,0:T(8,128)S(1)}, u32[]{:S(2)}, u32[]{:S(2)}) collective-permute-start(f32[16,3,16,128]{3,2,1,0:T(8,128)S(1)} %get-tuple-element.321), channel_id=1, source_target_pairs={{4,0},{8,4},{12,8},{16,12},{20,16},{24,20},{28,24},{0,28},{5,1},{9... | collective-permute-start | bytes 1179656 | tf_op jit(solution)/shard_map/while/body/eval_jaxpr/ppermute | solution.py:19
  80.3 12.0 %collective-permute-start = (f32[16,3,16,128]{3,2,1,0:T(8,128)S(1)}, f32[16,3,16,128]{3,2,1,0:T(8,128)S(1)}, u32[]{:S(2)}, u32[]{:S(2)}) collective-permute-start(f32[16,3,16,128]{3,2,1,0:T(8,128)S(1)} %get-tuple-element.321), channel_id=1, source_target_pairs={{4,0},{8,4},{12,8},{16,12},{20,16},{24,20},{28,24},{0,28},{5,1},{9... | collective-permute-start | bytes 1179656 | tf_op jit(solution)/shard_map/while/body/eval_jaxpr/ppermute | solution.py:19
  95.0 10.8 %all-to-all-start = ((f32[4,1,24576]{2,1,0:T(1,128)}), f32[4,1,24576]{2,1,0:T(1,128)S(1)}, u32[]{:S(2)}, u32[]{:S(2)}) async-start(f32[4,1,24576]{2,1,0:T(1,128)} %reshape.519), calls=%async_computation | async-start | bytes 786432 | tf_op jit(solution)/shard_map/all_to_all | solution.py:117
